TPU v7x, 32 devices: a whole 2x2x4 slice. The times are simulated.
32 devices in a mesh: ctx: 8 (over z, x), hd: 4 (over y, core).
Axes of the slice: x: 2, y: 2, z: 4, core: 2. Of those that a mesh axis runs over, the one named last changes fastest.
Arguments:
- queries: bfloat16 [4096, 3584], P(('ctx', 'hd')), may hold values from -8 to 8
- keys: bfloat16 [4096, 512], P(('ctx', 'hd')), may hold values from -8 to 8
- values: bfloat16 [4096, 512], P(('ctx', 'hd')), may hold values from -6 to 6
- window_blocks: int32 [32], replicated, may hold values from 1 to 16, as said below
- far_use: int32 [32, 4], replicated, may hold values from 0 to 1, as said below
Outputs:
- attended: bfloat16 [4096, 3584], P(('ctx', 'hd'))
Inputs may be any that keep to these rules, and one draw needn't show every extreme that they name: `window_blocks`: the value 16 occurs in every draw. far_use[b, e] is 0 wherever b < 16 * 2^e.
All inputs are finite; a program needn't handle non-finite values.
Results may differ from a plain program's by a relative error of at most 0.004.
Values may be sent and summed in bfloat16 or wider, within the bound.
A program may use at most 64 MiB of HBM per device.

v0:
```python
import functools
import math

import jax
import jax.numpy as jnp
from jax import lax
from jax.experimental import pallas as pl
from jax.experimental.pallas import tpu as pltpu
from jax.sharding import PartitionSpec as P

QUERY_HEADS = 28
KEY_VALUE_HEADS = 4
HEAD_SIZE = 128
BLOCK_TOKENS = 128
WIN = 16
NPOW = 4
GROUP = QUERY_HEADS // KEY_VALUE_HEADS
NEG = -1e30
EXP_SCALE = HEAD_SIZE ** (-0.5) * math.log2(math.e)

PLANE = 4
UNITS = WIN // 2 + 1


def kernel(sizes, wb_ref, far_ref, q_hbm, k_ref, v_ref, o_ref,
           q_ref, kv, top, total, accum, local_sem, send_sem, recv_sem, pair_send, pair_recv):
    ctx_size, hd_size = sizes
    devices = ctx_size * hd_size
    pairs = devices // 2
    far_steps = [WIN // 2 * 2**e for e in range(1, NPOW) if WIN // 2 * 2**e < pairs]
    me = lax.axis_index("ctx") * hd_size + lax.axis_index("hd")
    pair = me // 2
    core = me % 2
    place = pair % PLANE
    partner = me + 1 - 2 * core

    def at(device):
        return (device // hd_size, device % hd_size)

    copies = [
        pltpu.make_async_copy(k_ref, kv.at[0, core, 0], local_sem.at[0]),
        pltpu.make_async_copy(v_ref, kv.at[0, core, 1], local_sem.at[1]),
    ]
    load = pltpu.make_async_copy(q_hbm, q_ref, local_sem.at[2])
    for copy in copies:
        copy.start()
    load.start()

    barrier = pltpu.get_barrier_semaphore()
    steps = [PLANE] + far_steps

    def greet(device):
        pl.semaphore_signal(barrier, inc=1, device_id=at(device),
                            device_id_type=pl.DeviceIdType.MESH)

    greet(partner)
    cross = PLANE - 1 - 2 * place
    mates = [cross, 2 - 4 * (place // 2), 1 - 2 * (place % 2)]
    for delta in mates:
        greet(me + 2 * delta)
    for d in steps:
        @pl.when(pair + d < pairs)
        def _(d=d):
            greet(me + 2 * d)

        @pl.when(pair >= d)
        def _(d=d):
            greet(me - 2 * d)
    peers = jnp.int32(1 + len(mates))
    for d in steps:
        peers = peers + jnp.where(pair + d < pairs, 1, 0) + jnp.where(pair >= d, 1, 0)
    pl.semaphore_wait(barrier, peers)
    for copy in copies:
        copy.wait()

    def send(source, slot, device, number):
        return pltpu.make_async_remote_copy(
            src_ref=kv.at[source, core], dst_ref=kv.at[slot, core],
            send_sem=send_sem.at[number], recv_sem=recv_sem.at[slot],
            device_id=at(device), device_id_type=pl.DeviceIdType.MESH)

    def hand(unit):
        return pltpu.make_async_remote_copy(
            src_ref=kv.at[unit, core], dst_ref=kv.at[unit, core],
            send_sem=pair_send.at[unit], recv_sem=pair_recv.at[unit],
            device_id=at(partner), device_id_type=pl.DeviceIdType.MESH)

    def handed(unit):
        return pltpu.make_async_remote_copy(
            src_ref=kv.at[unit, 1 - core], dst_ref=kv.at[unit, 1 - core],
            send_sem=pair_send.at[unit], recv_sem=pair_recv.at[unit],
            device_id=at(partner), device_id_type=pl.DeviceIdType.MESH)

    first = 1 + 2 * (place % 2)
    second = PLANE - first

    own = [(pair + PLANE < pairs, 0, PLANE, me + 2 * PLANE)]
    own += [(delta > 0, 0, jnp.maximum(delta, 0), me + 2 * delta) for delta in mates]
    own += [(pair + d < pairs, 0, UNITS + i, me + 2 * d) for i, d in enumerate(far_steps)]
    near = [((pair >= PLANE) & (pair + PLANE < pairs), PLANE, 2 * PLANE, me + 2 * PLANE)]
    near += [((pair >= PLANE) & ((delta < 0) | (delta != cross)), PLANE, PLANE + delta,
              me + 2 * delta) for delta in mates]
    back = [((pair >= 2 * PLANE) & (delta < 0) & (delta != cross), 2 * PLANE,
             2 * PLANE + jnp.minimum(delta, 0), me + 2 * delta) for delta in mates]
    climb = [((pair >= first) & (pair + PLANE < pairs), first, first + PLANE, me + 2 * PLANE)]
    groups = []
    number = 0
    for group in (own, near, back, climb):
        groups.append([(cond, source, slot, device, number + i)
                       for i, (cond, source, slot, device) in enumerate(group)])
        number += len(group)

    def launch(group):
        for cond, source, slot, device, index in group:
            @pl.when(cond)
            def _(source=source, slot=slot, device=device, index=index):
                send(source, slot, device, index).start()

    launch(groups[0])
    hand(0).start()

    window = wb_ref[me]

    def update(units, group, mask):
        cols = pl.ds(pl.multiple_of(group * HEAD_SIZE, HEAD_SIZE), HEAD_SIZE)
        rows = 2 * BLOCK_TOKENS

        def gather(which):
            return jnp.concatenate(
                [kv[u, :, which, :, cols].reshape(rows, HEAD_SIZE) for u in units], axis=0)

        keys = gather(0)
        vals = gather(1)
        scores = []
        for j in range(GROUP):
            head = group * GROUP + j
            q = q_ref[:, pl.ds(pl.multiple_of(head * HEAD_SIZE, HEAD_SIZE), HEAD_SIZE)]
            scores.append(lax.dot_general(q, keys, (((1,), (1,)), ((), ())),
                                          preferred_element_type=jnp.float32))
        weights = []
        factors = []
        for j in range(GROUP):
            head = group * GROUP + j
            s = mask(scores[j])
            parts = [s[:, i:i + BLOCK_TOKENS] for i in range(0, s.shape[1], BLOCK_TOKENS)]
            peak = jnp.max(functools.reduce(jnp.maximum, parts), axis=-1, keepdims=True)
            before = top[head]
            now = jnp.maximum(before, peak)
            factor = jnp.exp2((before - now) * EXP_SCALE)
            exps = [jnp.exp2((part - now) * EXP_SCALE) for part in parts]
            weights.append(jnp.concatenate([p.astype(jnp.bfloat16) for p in exps], axis=1))
            factors.append(factor)
            top[head] = now
            total[head] = total[head] * factor + functools.reduce(jnp.add, exps)
        for j in range(GROUP):
            head = group * GROUP + j
            accum[head] = accum[head] * factors[j] + jnp.dot(
                weights[j], vals, preferred_element_type=jnp.float32)

    top[...] = jnp.full_like(top, NEG)
    total[...] = jnp.zeros_like(total)
    accum[...] = jnp.zeros_like(accum)
    load.wait()
    handed(0).wait_recv()

    row = lax.broadcasted_iota(jnp.int32, (BLOCK_TOKENS, 2 * BLOCK_TOKENS), 0)
    col = lax.broadcasted_iota(jnp.int32, (BLOCK_TOKENS, 2 * BLOCK_TOKENS), 1)
    edge = row + core * BLOCK_TOKENS
    floor = jnp.where(window > 1, 0, core * BLOCK_TOKENS)
    causal = (col <= edge) & (col >= floor)

    @pl.loop(0, KEY_VALUE_HEADS)
    def _(group):
        update((0,), group, lambda s: jnp.where(causal, s, NEG))

    def absorb(parts):
        bias = []
        for _, d, reach, flag in parts:
            for i in range(2):
                j = 2 * d + core - i
                ok = (pair >= d) & ((j < window) | ((j == reach) & (flag == 1)))
                bias.append(jnp.full((1, BLOCK_TOKENS), jnp.where(ok, 0.0, NEG), jnp.float32))
        bias = jnp.concatenate(bias, axis=1)

        @pl.loop(0, KEY_VALUE_HEADS)
        def _(group):
            update([part[0] for part in parts], group, lambda s: s + bias)

    @pl.loop(1, UNITS)
    def _(unit):
        @pl.when(pair < unit)
        def _():
            kv[unit] = jnp.zeros(kv.shape[1:], kv.dtype)

    def arrive(unit, group=None):
        @pl.when(pair >= unit)
        def _():
            send(0, unit, partner, 0).wait_recv()
            if group is not None:
                launch(group)
            hand(unit).start()

    flag = far_ref[0, me]

    def take(*units):
        for unit in units:
            @pl.when(pair >= unit)
            def _(unit=unit):
                handed(unit).wait_recv()

        @pl.when(pair >= functools.reduce(jnp.minimum, units))
        def _():
            absorb([(unit, unit, WIN, flag) for unit in units])

    half = PLANE // 2
    arrive(PLANE, groups[1])
    take(PLANE)
    arrive(2 * PLANE, groups[2])
    arrive(first, groups[3])
    take(2 * PLANE, first)
    arrive(half)
    arrive(second)
    take(half, second)
    arrive(PLANE + half)
    arrive(PLANE + second)
    take(PLANE + half, PLANE + second)
    arrive(PLANE + first)
    take(PLANE + first)

    for i, d in enumerate(far_steps):
        @pl.when(pair >= d)
        def _(i=i, d=d):
            send(0, UNITS + i, partner, 0).wait_recv()
            hand(UNITS + i).start()
            handed(UNITS + i).wait_recv()
            absorb([(UNITS + i, d, 2 * d, far_ref[i + 1, me])])

    @pl.loop(0, KEY_VALUE_HEADS)
    def _(group):
        for j in range(GROUP):
            head = group * GROUP + j
            whole_total = jnp.sum(total[head], axis=-1, keepdims=True)
            o_ref[:, pl.ds(pl.multiple_of(head * HEAD_SIZE, HEAD_SIZE), HEAD_SIZE)] = (
                accum[head] / whole_total).astype(o_ref.dtype)

    hand(0).wait_send()
    for unit, d in [(u, u) for u in range(1, UNITS)] + [
            (UNITS + i, d) for i, d in enumerate(far_steps)]:
        @pl.when(pair >= d)
        def _(unit=unit):
            hand(unit).wait_send()
    for group in groups:
        for cond, source, slot, device, index in group:
            @pl.when(cond)
            def _(source=source, slot=slot, device=device, index=index):
                send(source, slot, device, index).wait_send()


def per_device(sizes, queries, keys, values, window_blocks, far_use):
    tokens, kv_width = keys.shape
    assert tokens == BLOCK_TOKENS
    pairs = sizes[0] * sizes[1] // 2
    fars = len([e for e in range(1, NPOW) if WIN // 2 * 2**e < pairs])
    units = UNITS + fars
    vmem = pl.BlockSpec(memory_space=pltpu.VMEM)
    hbm = pl.BlockSpec(memory_space=pl.ANY)
    smem = pl.BlockSpec(memory_space=pltpu.SMEM)
    state = (QUERY_HEADS, BLOCK_TOKENS, HEAD_SIZE)
    return pl.pallas_call(
        functools.partial(kernel, sizes),
        out_shape=jax.ShapeDtypeStruct(queries.shape, queries.dtype),
        in_specs=[smem, smem, hbm, hbm, hbm],
        out_specs=vmem,
        scratch_shapes=[
            pltpu.VMEM(queries.shape, queries.dtype),
            pltpu.VMEM((units, 2, 2, tokens, kv_width), keys.dtype),
            pltpu.VMEM(state, jnp.float32),
            pltpu.VMEM(state, jnp.float32),
            pltpu.VMEM(state, jnp.float32),
            pltpu.SemaphoreType.DMA((3,)),
            pltpu.SemaphoreType.DMA((3 * PLANE + fars + 1,)),
            pltpu.SemaphoreType.DMA((units,)),
            pltpu.SemaphoreType.DMA((units,)),
            pltpu.SemaphoreType.DMA((units,)),
        ],
        compiler_params=pltpu.CompilerParams(
            collective_id=0, has_side_effects=True, vmem_limit_bytes=63 * 2**20),
    )(window_blocks, far_use.T, queries, keys, values)


def solution(mesh):
    placed = (P(("ctx", "hd"), None), P(("ctx", "hd"), None), P(("ctx", "hd"), None), P(), P())
    sizes = (mesh.shape["ctx"], mesh.shape["hd"])
    return jax.shard_map(
        functools.partial(per_device, sizes), mesh=mesh, in_specs=placed,
        out_specs=P(("ctx", "hd"), None), check_vma=False
    )
```

profile of v0, /device:TPU:16, one launch (start us, length us, event | category | flops | bytes accessed | tf_op | source)
XLA Modules:
  0.0 42.2 jit_solution(17673446603818906756)
XLA Ops:
  0.0 40.1 %shard_map.55 = bf16[128,3584]{1,0:T(8,128)(2,1)} custom-call(s32[32]{0:T(128)} %wb_ref.1, s32[4,32]{1,0:T(4,128)} %bitcast.1, bf16[128,3584]{1,0:T(8,128)(2,1)} %q_hbm.1, bf16[128,512]{1,0:T(8,128)(2,1)} %k_ref.1, bf16[128,512]{1,0:T(8,128)(2,1)} %v_ref.1), custom_call_target="tpu_custom_call" | custom-call | tf_op jit(solution)/shard_map/pallas_call | solution.py:269
  40.1 2.2 %copy.7 = bf16[128,3584]{1,0:T(8,128)(2,1)} copy(bf16[128,3584]{1,0:T(8,128)(2,1)} %shard_map.55) | data formatting | bytes 1835008
where the time goes:
time: 42.5 us; the launch traced here: 42.2 us
  Pallas kernels  40.1 us (94%)
  local copies, waits for them, and re-layouts  2.16 us (5%)
    pallas_call x1, Pallas kernels, per_device(): pl.pallas_call(functools.partial(kernel, sizes), out_shape=jax.ShapeDtype...  40.1 us
    unnamed x1, local copies, waits for them, and re-layouts  2.16 us

commit v1 on v0

v1 whole, which is shorter than its diff:
```python
import functools
import math

import jax
import jax.numpy as jnp
from jax import lax
from jax.experimental import pallas as pl
from jax.experimental.pallas import tpu as pltpu
from jax.sharding import PartitionSpec as P

QUERY_HEADS = 28
KEY_VALUE_HEADS = 4
HEAD_SIZE = 128
BLOCK_TOKENS = 128
WIN = 16
NPOW = 4
GROUP = QUERY_HEADS // KEY_VALUE_HEADS
NEG = -1e30
EXP_SCALE = HEAD_SIZE ** (-0.5) * math.log2(math.e)

PLANE = 4
UNITS = WIN // 2 + 1


def kernel(sizes, wb_ref, far_ref, q_hbm, k_hbm, v_hbm, o_ref,
           q_ref, kv, top, total, accum, local_sem, send_sem, recv_sem, pair_send, pair_recv):
    ctx_size, hd_size = sizes
    devices = ctx_size * hd_size
    pairs = devices // 2
    far_steps = [WIN // 2 * 2**e for e in range(1, NPOW) if WIN // 2 * 2**e < pairs]
    me = lax.axis_index("ctx") * hd_size + lax.axis_index("hd")
    pair = me // 2
    core = me % 2
    place = pair % PLANE
    partner = me + 1 - 2 * core

    def at(device):
        return (device // hd_size, device % hd_size)

    def local(group):
        cols = pl.ds(pl.multiple_of(group * HEAD_SIZE, HEAD_SIZE), HEAD_SIZE)
        return [pltpu.make_async_copy(ref.at[:, cols], kv.at[0, group, core, i],
                                      local_sem.at[group, i])
                for i, ref in enumerate((k_hbm, v_hbm))]

    load = pltpu.make_async_copy(q_hbm, q_ref, local_sem.at[KEY_VALUE_HEADS, 0])
    for group in range(KEY_VALUE_HEADS):
        for copy in local(group):
            copy.start()
    load.start()

    barrier = pltpu.get_barrier_semaphore()
    along_x = 2 - 4 * (place // 2)
    along_y = 1 - 2 * (place % 2)
    steps = [PLANE] + far_steps

    def greet(device):
        pl.semaphore_signal(barrier, inc=1, device_id=at(device),
                            device_id_type=pl.DeviceIdType.MESH)

    greet(partner)
    for delta in (along_x, along_y):
        greet(me + 2 * delta)
    for d in steps:
        @pl.when(pair + d < pairs)
        def _(d=d):
            greet(me + 2 * d)

        @pl.when(pair >= d)
        def _(d=d):
            greet(me - 2 * d)
    peers = jnp.int32(3)
    for d in steps:
        peers = peers + jnp.where(pair + d < pairs, 1, 0) + jnp.where(pair >= d, 1, 0)
    pl.semaphore_wait(barrier, peers)

    deltas = (PLANE, along_x, along_y)

    def send(direction, slot, group, target=None):
        delta = deltas[direction] if direction < 3 else far_steps[direction - 3]
        target = slot + delta if target is None else target
        return pltpu.make_async_remote_copy(
            src_ref=kv.at[slot, group, core], dst_ref=kv.at[target, group, core],
            send_sem=send_sem.at[direction, slot], recv_sem=recv_sem.at[target, group],
            device_id=at(me + 2 * delta), device_id_type=pl.DeviceIdType.MESH)

    def sent(direction, slot):
        pltpu.make_async_remote_copy(
            src_ref=kv.at[slot, :, core], dst_ref=kv.at[slot, :, core],
            send_sem=send_sem.at[direction, slot], recv_sem=recv_sem.at[slot, 0],
            device_id=at(partner), device_id_type=pl.DeviceIdType.MESH).wait_send()

    def arrived(slot, group):
        pltpu.make_async_remote_copy(
            src_ref=kv.at[slot, group, core], dst_ref=kv.at[slot, group, core],
            send_sem=send_sem.at[0, slot], recv_sem=recv_sem.at[slot, group],
            device_id=at(partner), device_id_type=pl.DeviceIdType.MESH).wait_recv()

    def hand(slot, group):
        return pltpu.make_async_remote_copy(
            src_ref=kv.at[slot, group, core], dst_ref=kv.at[slot, group, core],
            send_sem=pair_send.at[slot], recv_sem=pair_recv.at[slot, group],
            device_id=at(partner), device_id_type=pl.DeviceIdType.MESH)

    def given(slot):
        pltpu.make_async_remote_copy(
            src_ref=kv.at[slot, :, core], dst_ref=kv.at[slot, :, core],
            send_sem=pair_send.at[slot], recv_sem=pair_recv.at[slot, 0],
            device_id=at(partner), device_id_type=pl.DeviceIdType.MESH).wait_send()

    def handed(slot, group):
        pltpu.make_async_remote_copy(
            src_ref=kv.at[slot, group, 1 - core], dst_ref=kv.at[slot, group, 1 - core],
            send_sem=pair_send.at[slot], recv_sem=pair_recv.at[slot, group],
            device_id=at(partner), device_id_type=pl.DeviceIdType.MESH).wait_recv()

    UP, X, Y = 0, 1, 2
    above = pair + PLANE < pairs
    own = [(UP, above), (X, along_x > 0), (Y, along_y > 0)]
    own += [(3 + i, pair + d < pairs) for i, d in enumerate(far_steps)]

    for group in range(KEY_VALUE_HEADS):
        for copy in local(group):
            copy.wait()
        for direction, cond in own[:3]:
            @pl.when(cond)
            def _(direction=direction, group=group):
                send(direction, 0, group).start()
        hand(0, group).start()
    for i in range(len(far_steps)):
        @pl.when(own[3 + i][1])
        def _(i=i):
            for group in range(KEY_VALUE_HEADS):
                send(3 + i, 0, group, UNITS + i).start()

    window = wb_ref[me]

    def pick(*values):
        out = jnp.int32(values[-1])
        for i in range(PLANE - 1):
            out = jnp.where(place == i, values[i], out)
        return out

    high = place >= 2
    odd = place % 2 == 1
    stage = [
        [(PLANE, [(UP, above), (X, None), (Y, None)]), (2, [(Y, high)])],
        [(pick(3, 1, 1, 1), [(X, place == 0)]), (2 * PLANE, [(X, high), (Y, odd)])],
        [(6, [(Y, jnp.logical_not(high))]), (pick(7, 5, 3, 5), [(X, place > 0)])],
        [(2 * place + 1, []), (pick(5, 7, 7, 3), [])],
    ]

    def handle(number, group):
        for slot, forwards in stage[number]:
            @pl.when(pair >= slot)
            def _(slot=slot, forwards=forwards):
                arrived(slot, group)
                for direction, cond in forwards:
                    if cond is None:
                        send(direction, slot, group).start()
                    else:
                        @pl.when(cond)
                        def _(direction=direction):
                            send(direction, slot, group).start()
                hand(slot, group).start()

    def update(units, group, mask):
        rows = 2 * BLOCK_TOKENS

        def gather(which):
            return jnp.concatenate(
                [kv[u, group, :, which].reshape(rows, HEAD_SIZE) for u in units], axis=0)

        keys = gather(0)
        vals = gather(1)
        scores = []
        for j in range(GROUP):
            head = group * GROUP + j
            q = q_ref[:, pl.ds(pl.multiple_of(head * HEAD_SIZE, HEAD_SIZE), HEAD_SIZE)]
            scores.append(lax.dot_general(q, keys, (((1,), (1,)), ((), ())),
                                          preferred_element_type=jnp.float32))
        weights = []
        factors = []
        for j in range(GROUP):
            head = group * GROUP + j
            s = mask(scores[j])
            parts = [s[:, i:i + BLOCK_TOKENS] for i in range(0, s.shape[1], BLOCK_TOKENS)]
            peak = jnp.max(functools.reduce(jnp.maximum, parts), axis=-1, keepdims=True)
            before = top[head]
            now = jnp.maximum(before, peak)
            factor = jnp.exp2((before - now) * EXP_SCALE)
            exps = [jnp.exp2((part - now) * EXP_SCALE) for part in parts]
            weights.append(jnp.concatenate([p.astype(jnp.bfloat16) for p in exps], axis=1))
            factors.append(factor)
            top[head] = now
            total[head] = total[head] * factor + functools.reduce(jnp.add, exps)
        for j in range(GROUP):
            head = group * GROUP + j
            accum[head] = accum[head] * factors[j] + jnp.dot(
                weights[j], vals, preferred_element_type=jnp.float32)

    top[...] = jnp.full_like(top, NEG)
    total[...] = jnp.zeros_like(total)
    accum[...] = jnp.zeros_like(accum)

    @pl.loop(1, UNITS)
    def _(unit):
        @pl.when(pair < unit)
        def _():
            kv[unit] = jnp.zeros(kv.shape[1:], kv.dtype)

    load.wait()

    row = lax.broadcasted_iota(jnp.int32, (BLOCK_TOKENS, 2 * BLOCK_TOKENS), 0)
    col = lax.broadcasted_iota(jnp.int32, (BLOCK_TOKENS, 2 * BLOCK_TOKENS), 1)
    edge = row + core * BLOCK_TOKENS
    floor = jnp.where(window > 1, 0, core * BLOCK_TOKENS)
    causal = (col <= edge) & (col >= floor)

    @pl.loop(0, KEY_VALUE_HEADS)
    def _(group):
        handed(0, group)
        update((0,), group, lambda s: jnp.where(causal, s, NEG))
        handle(0, group)

    def absorb(parts, group):
        bias = []
        for _, d, reach, flag in parts:
            for i in range(2):
                j = 2 * d + core - i
                ok = (pair >= d) & ((j < window) | ((j == reach) & (flag == 1)))
                bias.append(jnp.full((1, BLOCK_TOKENS), jnp.where(ok, 0.0, NEG), jnp.float32))
        bias = jnp.concatenate(bias, axis=1)
        update([part[0] for part in parts], group, lambda s: s + bias)

    flag = far_ref[0, me]

    for number in range(len(stage)):
        slots = [slot for slot, _ in stage[number]]

        @pl.loop(0, KEY_VALUE_HEADS)
        def _(group, number=number, slots=slots):
            @pl.when(pair >= functools.reduce(jnp.minimum, slots))
            def _():
                for slot in slots:
                    @pl.when(pair >= slot)
                    def _(slot=slot):
                        handed(slot, group)
                absorb([(slot, slot, WIN, flag) for slot in slots], group)

            if number + 1 < len(stage):
                handle(number + 1, group)

    for i, d in enumerate(far_steps):
        @pl.when(pair >= d)
        def _(i=i, d=d):
            @pl.loop(0, KEY_VALUE_HEADS)
            def _(group):
                arrived(UNITS + i, group)
                hand(UNITS + i, group).start()
                handed(UNITS + i, group)
                absorb([(UNITS + i, d, 2 * d, far_ref[i + 1, me])], group)

    @pl.loop(0, KEY_VALUE_HEADS)
    def _(group):
        for j in range(GROUP):
            head = group * GROUP + j
            whole_total = jnp.sum(total[head], axis=-1, keepdims=True)
            o_ref[:, pl.ds(pl.multiple_of(head * HEAD_SIZE, HEAD_SIZE), HEAD_SIZE)] = (
                accum[head] / whole_total).astype(o_ref.dtype)

    for direction, cond in own:
        @pl.when(cond)
        def _(direction=direction):
            sent(direction, 0)
    given(0)
    for step in stage:
        for slot, forwards in step:
            @pl.when(pair >= slot)
            def _(slot=slot, forwards=forwards):
                for direction, cond in forwards:
                    if cond is None:
                        sent(direction, slot)
                    else:
                        @pl.when(cond)
                        def _(direction=direction):
                            sent(direction, slot)
                given(slot)
    for i, d in enumerate(far_steps):
        @pl.when(pair >= d)
        def _(i=i):
            given(UNITS + i)


def per_device(sizes, queries, keys, values, window_blocks, far_use):
    tokens, kv_width = keys.shape
    assert tokens == BLOCK_TOKENS
    pairs = sizes[0] * sizes[1] // 2
    fars = len([e for e in range(1, NPOW) if WIN // 2 * 2**e < pairs])
    units = UNITS + fars
    vmem = pl.BlockSpec(memory_space=pltpu.VMEM)
    hbm = pl.BlockSpec(memory_space=pl.ANY)
    smem = pl.BlockSpec(memory_space=pltpu.SMEM)
    state = (QUERY_HEADS, BLOCK_TOKENS, HEAD_SIZE)
    return pl.pallas_call(
        functools.partial(kernel, sizes),
        out_shape=jax.ShapeDtypeStruct(queries.shape, queries.dtype),
        in_specs=[smem, smem, hbm, hbm, hbm],
        out_specs=vmem,
        scratch_shapes=[
            pltpu.VMEM(queries.shape, queries.dtype),
            pltpu.VMEM((units, KEY_VALUE_HEADS, 2, 2, tokens, HEAD_SIZE), keys.dtype),
            pltpu.VMEM(state, jnp.float32),
            pltpu.VMEM(state, jnp.float32),
            pltpu.VMEM(state, jnp.float32),
            pltpu.SemaphoreType.DMA((KEY_VALUE_HEADS + 1, 2)),
            pltpu.SemaphoreType.DMA((3 + fars, units)),
            pltpu.SemaphoreType.DMA((units, KEY_VALUE_HEADS)),
            pltpu.SemaphoreType.DMA((units,)),
            pltpu.SemaphoreType.DMA((units, KEY_VALUE_HEADS)),
        ],
        compiler_params=pltpu.CompilerParams(
            collective_id=0, has_side_effects=True, vmem_limit_bytes=63 * 2**20),
    )(window_blocks, far_use.T, queries, keys, values)


def solution(mesh):
    placed = (P(("ctx", "hd"), None), P(("ctx", "hd"), None), P(("ctx", "hd"), None), P(), P())
    sizes = (mesh.shape["ctx"], mesh.shape["hd"])
    return jax.shard_map(
        functools.partial(per_device, sizes), mesh=mesh, in_specs=placed,
        out_specs=P(("ctx", "hd"), None), check_vma=False
    )
```

time: 42.5 us -> 36.8 us (0.87)
  Pallas kernels: 40.1 us -> 34.4 us
    pallas_call x1, Pallas kernels: 40.1 us -> 34.4 us  [per_device(): pl.pallas_call(functools.partial(kernel, sizes), out_shape=jax.ShapeDtype...]
where the time goes in v1:
time: 36.8 us; the launch traced here: 36.6 us
  Pallas kernels  34.4 us (93%)
  local copies, waits for them, and re-layouts  2.16 us (6%)
    pallas_call x1, Pallas kernels, per_device(): pl.pallas_call(functools.partial(kernel, sizes), out_shape=jax.ShapeDtype...  34.4 us
    unnamed x1, local copies, waits for them, and re-layouts  2.16 us

profile of v1, /device:TPU:16, one launch (start us, length us, event | category | flops | bytes accessed | tf_op | source)
XLA Modules:
  0.0 36.6 jit_solution(3269096379329925859)
XLA Ops:
  0.0 34.4 %shard_map.55 = bf16[128,3584]{1,0:T(8,128)(2,1)} custom-call(s32[32]{0:T(128)} %wb_ref.1, s32[4,32]{1,0:T(4,128)} %bitcast.1, bf16[128,3584]{1,0:T(8,128)(2,1)} %q_hbm.1, bf16[128,512]{1,0:T(8,128)(2,1)} %k_hbm.1, bf16[128,512]{1,0:T(8,128)(2,1)} %v_hbm.1), custom_call_target="tpu_custom_call" | custom-call | tf_op jit(solution)/shard_map/pallas_call | solution.py:305
  34.4 2.2 %copy.7 = bf16[128,3584]{1,0:T(8,128)(2,1)} copy(bf16[128,3584]{1,0:T(8,128)(2,1)} %shard_map.55) | data formatting | bytes 1835008
